TPU v7x, 32 devices: a whole 2x2x4 slice. The times are simulated.
32 devices in a mesh: batch: 4 (over x, core), head: 8 (over z, y).
Axes of the slice: x: 2, y: 2, z: 4, core: 2. Of those that a mesh axis runs over, the one named last changes fastest.
Arguments:
- tokens: bfloat16 [5120, 2048], P('batch'), may hold values from -6 to 6
- segment_ids: int32 [5120], P('batch'), may hold values from 0 to 6, as said below
- norm1_gain: bfloat16 [2048], P('batch'), may hold values from 0.25 to 1.75
- w_query: bfloat16 [2048, 1024], P('batch', 'head'), may hold values from -0.125 to 0.125
- w_key: bfloat16 [2048, 512], P('batch', 'head'), may hold values from -0.125 to 0.125
- w_value: bfloat16 [2048, 512], P('batch', 'head'), may hold values from -0.125 to 0.125
- w_gate: bfloat16 [2048, 1024], P('batch', 'head'), may hold values from -0.125 to 0.125
- w_out: bfloat16 [1024, 2048], P('head', 'batch'), may hold values from -4 to 4
- norm2_gain: bfloat16 [2048], P('batch'), may hold values from 0.25 to 1.75
- w_mlp_gate: bfloat16 [2048, 6144], P('batch', 'head'), may hold values from -0.125 to 0.125
- w_mlp_up: bfloat16 [2048, 6144], P('batch', 'head'), may hold values from -0.125 to 0.125
- w_down: bfloat16 [6144, 2048], P('head', 'batch'), may hold values from -0.078125 to 0.078125
- out_grad: bfloat16 [5120, 2048], P('batch'), may hold values from -6 to 6
Outputs:
- output: bfloat16 [5120, 2048], P('batch')
- d_tokens: bfloat16 [5120, 2048], P('batch')
- d_norm1_gain: float32 [2048], P('batch')
- d_w_query: float32 [2048, 1024], P('batch', 'head')
- d_w_key: float32 [2048, 512], P('batch', 'head')
- d_w_value: float32 [2048, 512], P('batch', 'head')
- d_w_gate: float32 [2048, 1024], P('batch', 'head')
- d_w_out: float32 [1024, 2048], P('head', 'batch')
- d_norm2_gain: float32 [2048], P('batch')
- d_w_mlp_gate: float32 [2048, 6144], P('batch', 'head')
- d_w_mlp_up: float32 [2048, 6144], P('batch', 'head')
- d_w_down: float32 [6144, 2048], P('head', 'batch')
Inputs may be any that keep to these rules, and one draw needn't show every extreme that they name: `segment_ids`: segment ids never fall along the packed batch and every id from 0 to 6 occurs.
All inputs are finite; a program needn't handle non-finite values.
Results may differ from a plain program's by a relative error of at most 0.02.
Values may be sent and summed in bfloat16 or wider, within the bound.
A program may use at most 256 MiB of HBM per device.

v0:
```python
import math
import jax
import jax.numpy as jnp
from jax import lax
from jax.sharding import PartitionSpec as P

EPSILON = 1e-06
MASKED = -1e30


def from_partner(block, axis, stride):
    count = lax.axis_size(axis)
    route = []
    for low in range(count):
        high = low | 1 << stride
        if high != low and high < count:
            route += [(low, high), (high, low)]
    return lax.ppermute(block, axis, route)


def matmul(left, right):
    return jnp.dot(left, right, preferred_element_type=jnp.float32)


def rows_inner(left, right):
    return lax.dot_general(
        left, right, (((0,), (0,)), ((), ())), preferred_element_type=jnp.float32
    )


def cols_inner(left, right):
    return lax.dot_general(
        left, right, (((1,), (1,)), ((), ())), preferred_element_type=jnp.float32
    )


def rms_scale(values):
    return lax.rsqrt(jnp.mean(values * values, axis=1, keepdims=True) + EPSILON)


def keep_same(state):
    return state


def per_device(
    tokens,
    segment_ids,
    norm1_gain,
    w_query,
    w_key,
    w_value,
    w_gate,
    w_out,
    norm2_gain,
    w_mlp_gate,
    w_mlp_up,
    w_down,
    out_grad,
):
    gathered = (
        lax.all_gather(norm1_gain, "batch", axis=0, tiled=True),
        lax.all_gather(w_query, "batch", axis=0, tiled=True),
        lax.all_gather(w_key, "batch", axis=0, tiled=True),
        lax.all_gather(w_value, "batch", axis=0, tiled=True),
        lax.all_gather(w_gate, "batch", axis=0, tiled=True),
        lax.all_gather(w_out, "batch", axis=1, tiled=True),
        lax.all_gather(norm2_gain, "batch", axis=0, tiled=True),
        lax.all_gather(w_mlp_gate, "batch", axis=0, tiled=True),
        lax.all_gather(w_mlp_up, "batch", axis=0, tiled=True),
        lax.all_gather(w_down, "batch", axis=1, tiled=True),
    )
    (
        gain_one,
        query_full,
        key_full,
        value_full,
        gate_full,
        out_full,
        gain_two,
        mgate_full,
        mup_full,
        down_full,
    ) = gathered
    gain_one = gain_one.astype(jnp.float32)
    gain_two = gain_two.astype(jnp.float32)
    row_count = tokens.shape[0]
    head_size = query_full.shape[1]
    half_width = key_full.shape[1]
    scale_factor = 1.0 / math.sqrt(head_size)
    positions = lax.axis_index("batch") * row_count + jnp.arange(row_count, dtype=jnp.int32)
    inputs = tokens.astype(jnp.float32)
    recip_one = rms_scale(inputs)
    normed_one = (inputs * recip_one * gain_one).astype(jnp.bfloat16)
    queries = matmul(normed_one, query_full).astype(jnp.bfloat16)
    kv_half = matmul(normed_one, jnp.concatenate([key_full, value_full], axis=1)).astype(
        jnp.bfloat16
    )
    partner = from_partner(kv_half, "head", 0)
    lower_half = lax.axis_index("head") % 2 == 0
    own_key, own_value = (kv_half[:, :half_width], kv_half[:, half_width:])
    mate_key, mate_value = (partner[:, :half_width], partner[:, half_width:])
    keys_full = jnp.where(
        lower_half, jnp.concatenate([own_key, mate_key], 1), jnp.concatenate([mate_key, own_key], 1)
    )
    values_full = jnp.where(
        lower_half,
        jnp.concatenate([own_value, mate_value], 1),
        jnp.concatenate([mate_value, own_value], 1),
    )
    kv_local = jnp.concatenate([keys_full, values_full], axis=1)
    kv_all, seg_all = (
        lax.all_gather(kv_local, "batch", axis=0, tiled=True),
        lax.all_gather(segment_ids, "batch", axis=0, tiled=True),
    )
    group_total = kv_all.shape[0] // row_count
    per_block = max(
        (
            step
            for step in range(1, group_total + 1)
            if group_total % step == 0 and step * row_count <= max(row_count, 1024)
        )
    )
    block_rows = per_block * row_count
    block_total = group_total // per_block

    def block_parts(block_index):
        first_row = block_index * block_rows
        key_block = kv_all[first_row : first_row + block_rows, :head_size]
        value_block = kv_all[first_row : first_row + block_rows, head_size:]
        seg_block = seg_all[first_row : first_row + block_rows]
        key_pos = first_row + jnp.arange(block_rows, dtype=jnp.int32)
        allowed = (segment_ids[:, None] == seg_block[None, :]) & (
            key_pos[None, :] <= positions[:, None]
        )
        scores = cols_inner(queries, key_block) * scale_factor
        return (scores, allowed, key_block, value_block)

    def is_live(block_index):
        first_row = block_index * block_rows
        return (first_row <= positions[-1]) & (
            seg_all[first_row + block_rows - 1] >= segment_ids[0]
        )

    run_max = jnp.full((row_count,), MASKED, jnp.float32)
    run_sum = jnp.zeros((row_count,), jnp.float32)
    for block_index in range(block_total):

        def grow(state, block_index=block_index):
            old_max, old_sum = state
            scores, allowed, key_block, value_block = block_parts(block_index)
            new_max = jnp.maximum(old_max, jnp.max(jnp.where(allowed, scores, MASKED), axis=1))
            weights = jnp.where(allowed, jnp.exp(scores - new_max[:, None]), 0.0)
            return (new_max, old_sum * jnp.exp(old_max - new_max) + jnp.sum(weights, axis=1))

        run_max, run_sum = lax.cond(is_live(block_index), grow, keep_same, (run_max, run_sum))
    log_total = run_max + jnp.log(run_sum)

    def probs_of(block_index):
        scores, allowed, key_block, value_block = block_parts(block_index)
        return (
            jnp.where(allowed, jnp.exp(scores - log_total[:, None]), 0.0),
            key_block,
            value_block,
        )

    attended = jnp.zeros((row_count, head_size), jnp.float32)
    for block_index in range(block_total):

        def accumulate(running, block_index=block_index):
            probs, key_block, value_block = probs_of(block_index)
            return running + matmul(probs.astype(jnp.bfloat16), value_block)

        attended = lax.cond(is_live(block_index), accumulate, keep_same, attended)
    gate_vals = jax.nn.sigmoid(matmul(normed_one, gate_full))
    mixed = (attended * gate_vals).astype(jnp.bfloat16)
    attn_part = matmul(mixed, out_full)
    resid = inputs + lax.psum(attn_part, "head")
    recip_two = rms_scale(resid)
    normed_two = (resid * recip_two * gain_two).astype(jnp.bfloat16)
    gate_pre = matmul(normed_two, mgate_full)
    up_pre = matmul(normed_two, mup_full)
    sig_gate = jax.nn.sigmoid(gate_pre)
    silu_gate = gate_pre * sig_gate
    hidden = (silu_gate * up_pre).astype(jnp.bfloat16)
    mlp_part = matmul(hidden, down_full)
    d_down = rows_inner(hidden, out_grad)
    d_hidden = cols_inner(out_grad, down_full)
    d_gate_pre = (d_hidden * up_pre * sig_gate * (1.0 + gate_pre * (1.0 - sig_gate))).astype(
        jnp.bfloat16
    )
    d_up_pre = (d_hidden * silu_gate).astype(jnp.bfloat16)
    d_mgate = rows_inner(normed_two, d_gate_pre)
    d_mup = rows_inner(normed_two, d_up_pre)
    dn2_part = cols_inner(d_gate_pre, mgate_full) + cols_inner(d_up_pre, mup_full)
    mlp_total = lax.psum(mlp_part.astype(jnp.bfloat16), "head").astype(jnp.float32)
    output = (resid + mlp_total).astype(jnp.bfloat16)
    d_normed_two = lax.psum(dn2_part.astype(jnp.bfloat16), "head").astype(jnp.float32)
    gain_two_full = jnp.sum(d_normed_two * resid * recip_two, axis=0)
    gain_two_term = jnp.where(
        lax.axis_index("head") == 0, gain_two_full, jnp.zeros_like(gain_two_full)
    )
    weighted_two = gain_two * d_normed_two
    d_resid = (
        out_grad.astype(jnp.float32)
        + recip_two * weighted_two
        - resid * recip_two**3 * jnp.mean(weighted_two * resid, axis=1, keepdims=True)
    )
    d_resid_low = d_resid.astype(jnp.bfloat16)
    d_out = rows_inner(mixed, d_resid_low)
    d_mixed = cols_inner(d_resid_low, out_full)
    d_attended = (d_mixed * gate_vals).astype(jnp.bfloat16)
    d_gate_logit = (d_mixed * attended * gate_vals * (1.0 - gate_vals)).astype(jnp.bfloat16)
    delta = jnp.zeros((row_count,), jnp.float32)
    for block_index in range(block_total):

        def delta_add(running, block_index=block_index):
            probs, key_block, value_block = probs_of(block_index)
            return running + jnp.sum(probs * cols_inner(d_attended, value_block), axis=1)

        delta = lax.cond(is_live(block_index), delta_add, keep_same, delta)
    d_queries = jnp.zeros((row_count, head_size), jnp.float32)
    grad_pieces = []
    for block_index in range(block_total):

        def block_grads(running, block_index=block_index):
            probs, key_block, value_block = probs_of(block_index)
            d_probs = cols_inner(d_attended, value_block)
            d_scores = (probs * (d_probs - delta[:, None]) * scale_factor).astype(jnp.bfloat16)
            d_key_block = rows_inner(d_scores, queries)
            d_value_block = rows_inner(probs.astype(jnp.bfloat16), d_attended)
            return (
                running + matmul(d_scores, key_block),
                jnp.concatenate([d_key_block, d_value_block], axis=1),
            )

        def block_empty(running):
            return (running, jnp.zeros((block_rows, 2 * head_size), jnp.float32))

        d_queries, grad_piece = lax.cond(is_live(block_index), block_grads, block_empty, d_queries)
        grad_pieces.append(grad_piece)
    d_kv_all = jnp.concatenate(grad_pieces, axis=0)
    d_kv_own = lax.psum_scatter(
        d_kv_all.astype(jnp.bfloat16), "batch", scatter_dimension=0, tiled=True
    ).astype(jnp.float32)
    d_kv_mate = from_partner(d_kv_own.astype(jnp.bfloat16), "head", 0).astype(d_kv_own.dtype)
    d_kv_low = (d_kv_own + d_kv_mate).astype(jnp.bfloat16)
    d_key_half = jnp.where(lower_half, d_kv_low[:, :half_width], d_kv_low[:, half_width:head_size])
    d_value_half = jnp.where(
        lower_half,
        d_kv_low[:, head_size : head_size + half_width],
        d_kv_low[:, head_size + half_width :],
    )
    d_queries_low = d_queries.astype(jnp.bfloat16)
    d_query_w = rows_inner(normed_one, d_queries_low)
    d_key_w = rows_inner(normed_one, d_key_half)
    d_value_w = rows_inner(normed_one, d_value_half)
    d_gate_w = rows_inner(normed_one, d_gate_logit)
    dn1_part = (
        cols_inner(d_queries_low, query_full)
        + cols_inner(d_key_half, key_full)
        + cols_inner(d_value_half, value_full)
        + cols_inner(d_gate_logit, gate_full)
    )
    d_normed_one, d_gain_two = (
        lax.psum(dn1_part.astype(jnp.bfloat16), "head").astype(jnp.float32),
        lax.psum(gain_two_term.astype(jnp.bfloat16), "head").astype(jnp.float32),
    )
    d_gain_one = jnp.sum(d_normed_one * inputs * recip_one, axis=0)
    weighted_one = gain_one * d_normed_one
    d_tokens = (
        d_resid
        + recip_one * weighted_one
        - inputs * recip_one**3 * jnp.mean(weighted_one * inputs, axis=1, keepdims=True)
    ).astype(jnp.bfloat16)
    summed = (
        lax.psum_scatter(
            d_gain_one.astype(jnp.bfloat16), "batch", scatter_dimension=0, tiled=True
        ).astype(jnp.float32),
        lax.psum_scatter(
            d_query_w.astype(jnp.bfloat16), "batch", scatter_dimension=0, tiled=True
        ).astype(jnp.float32),
        lax.psum_scatter(
            d_key_w.astype(jnp.bfloat16), "batch", scatter_dimension=0, tiled=True
        ).astype(jnp.float32),
        lax.psum_scatter(
            d_value_w.astype(jnp.bfloat16), "batch", scatter_dimension=0, tiled=True
        ).astype(jnp.float32),
        lax.psum_scatter(
            d_gate_w.astype(jnp.bfloat16), "batch", scatter_dimension=0, tiled=True
        ).astype(jnp.float32),
        lax.psum_scatter(
            d_out.astype(jnp.bfloat16), "batch", scatter_dimension=1, tiled=True
        ).astype(jnp.float32),
        lax.psum_scatter(
            d_gain_two.astype(jnp.bfloat16), "batch", scatter_dimension=0, tiled=True
        ).astype(jnp.float32),
        lax.psum_scatter(
            d_mgate.astype(jnp.bfloat16), "batch", scatter_dimension=0, tiled=True
        ).astype(jnp.float32),
        lax.psum_scatter(
            d_mup.astype(jnp.bfloat16), "batch", scatter_dimension=0, tiled=True
        ).astype(jnp.float32),
        lax.psum_scatter(
            d_down.astype(jnp.bfloat16), "batch", scatter_dimension=1, tiled=True
        ).astype(jnp.float32),
    )
    return (
        output,
        d_tokens,
        summed[0],
        summed[1],
        summed[2],
        summed[3],
        summed[4],
        summed[5],
        summed[6],
        summed[7],
        summed[8],
        summed[9],
    )


def solution(mesh):
    return jax.shard_map(
        per_device,
        mesh=mesh,
        in_specs=(
            P("batch", None),
            P("batch"),
            P("batch"),
            P("batch", "head"),
            P("batch", "head"),
            P("batch", "head"),
            P("batch", "head"),
            P("head", "batch"),
            P("batch"),
            P("batch", "head"),
            P("batch", "head"),
            P("head", "batch"),
            P("batch", None),
        ),
        out_specs=(
            P("batch", None),
            P("batch", None),
            P("batch"),
            P("batch", "head"),
            P("batch", "head"),
            P("batch", "head"),
            P("batch", "head"),
            P("head", "batch"),
            P("batch"),
            P("batch", "head"),
            P("batch", "head"),
            P("head", "batch"),
        ),
        check_vma=False,
    )
```

profile of v0, /device:TPU:0, one launch (start us, length us, event | category | flops | bytes accessed | tf_op | source)
XLA Modules:
  0.0 1581.4 jit_solution(1215481020769771091)
XLA Ops:
  38.2 8.3 collective-permute-done
  62.4 10.5 all_gather.41
  92.7 9.2 conditional.16
  124.7 57.2 %all-gather.2 = bf16[4,1,512]{2,1,0:T(2,128)(2,1)S(1)} all-gather(bf16[1,1,512]{2,1,0:T(2,128)(2,1)S(1)} %reshape.212), channel_id=1, replica_groups=mesh['batch'=4,'head'=8] {'batch'}, dimensions={0}, use_global_device_ids=true | all-gather | bytes 5120 | tf_op jit(solution)/shard_map/all_gather | solution.py:67
  181.9 321.6 %all-reduce.8.cloned.1.call-done = f32[1280,2048]{1,0:T(8,128)} async-done(((f32[1280,2048]{1,0:T(8,128)}), f32[1280,2048]{1,0:T(8,128)}) %all-reduce.8.cloned.1.call-update) | async-done | bytes 10485776 | tf_op jit(solution)/shard_map/psum | solution.py:177
  503.6 11.1 multiply_reduce_fusion
  522.0 10.8 all-gather.12.cloned.1.call-done
  532.8 9.6 fusion.161
  542.4 20.5 %all-gather.10.cloned.1.call-done = bf16[2048,768]{1,0:T(8,128)(2,1)} async-done(((bf16[512,768]{1,0:T(8,128)(2,1)}), bf16[2048,768]{1,0:T(8,128)(2,1)}) %all-gather.10.cloned.1.call-update) | async-done | bytes 3145744 | tf_op jit(solution)/shard_map/all_gather | solution.py:68
  562.9 9.7 fusion.160
  572.6 20.4 %all-gather.14.cloned.1.call-done = bf16[768,2048]{1,0:T(8,128)(2,1)} async-done(((bf16[768,512]{1,0:T(8,128)(2,1)}), bf16[768,2048]{1,0:T(8,128)(2,1)}) %all-gather.14.cloned.1.call-update) | async-done | bytes 3145744 | tf_op jit(solution)/shard_map/all_gather | solution.py:70
  592.9 13.6 multiply_convert_fusion.1
  619.2 183.7 %all-reduce.10.cloned.1.call-done = bf16[1280,2048]{1,0:T(8,128)(2,1)} async-done(((bf16[1280,2048]{1,0:T(8,128)(2,1)}), bf16[1280,2048]{1,0:T(8,128)(2,1)}) %all-reduce.10.cloned.1.call-update) | async-done | bytes 5242896 | tf_op jit(solution)/shard_map/psum | solution.py:197
  802.9 9.4 fusion.124
  824.3 8.2 conditional.24
  832.8 13.0 conditional.28
  855.9 8.2 convolution_convert_fusion.1
  864.4 9.1 convolution_convert_fusion.2
  873.6 9.1 convolution_convert_fusion.3
  901.5 44.9 %reduce-scatter.10.cloned.1.call-done = bf16[1280,256]{0,1:T(8,128)(2,1)} async-done(((bf16[5120,256]{0,1:T(8,128)(2,1)}), bf16[1280,256]{0,1:T(8,128)(2,1)}) %reduce-scatter.10.cloned.1.call-update) | async-done | bytes 655376 | tf_op jit(solution)/shard_map/reduce_scatter | solution.py:242
  983.1 13.4 add_convert_fusion
  1001.0 26.6 %reduce-scatter.24.cloned.1.call-done = bf16[512,768]{1,0:T(8,128)(2,1)} async-done(((bf16[2048,768]{1,0:T(8,128)(2,1)}), bf16[512,768]{1,0:T(8,128)(2,1)}) %reduce-scatter.24.cloned.1.call-update) | async-done | bytes 786448 | tf_op jit(solution)/shard_map/reduce_scatter | solution.py:300
  1030.0 38.0 %reduce-scatter.22.cloned.1.call-done = bf16[512,768]{1,0:T(8,128)(2,1)} async-done(((bf16[2048,768]{1,0:T(8,128)(2,1)}), bf16[512,768]{1,0:T(8,128)(2,1)}) %reduce-scatter.22.cloned.1.call-update) | async-done | bytes 786448 | tf_op jit(solution)/shard_map/reduce_scatter | solution.py:297
  1070.4 22.0 %reduce-scatter.20.cloned.1.call-done = bf16[128,512]{1,0:T(8,128)(2,1)} async-done(((bf16[128,2048]{1,0:T(8,128)(2,1)}), bf16[128,512]{1,0:T(8,128)(2,1)}) %reduce-scatter.20.cloned.1.call-update) | async-done | bytes 131088 | tf_op jit(solution)/shard_map/reduce_scatter | solution.py:291
  1094.0 22.4 %reduce-scatter.18.cloned.1.call-done = bf16[512,128]{1,0:T(8,128)(2,1)} async-done(((bf16[2048,128]{1,0:T(8,128)(2,1)}), bf16[512,128]{1,0:T(8,128)(2,1)}) %reduce-scatter.18.cloned.1.call-update) | async-done | bytes 131088 | tf_op jit(solution)/shard_map/reduce_scatter | solution.py:288
  1118.0 22.7 %reduce-scatter.12.cloned.1.call-done = bf16[512,128]{1,0:T(8,128)(2,1)} async-done(((bf16[2048,128]{1,0:T(8,128)(2,1)}), bf16[512,128]{1,0:T(8,128)(2,1)}) %reduce-scatter.12.cloned.1.call-update) | async-done | bytes 131088 | tf_op jit(solution)/shard_map/reduce_scatter | solution.py:279
  1142.4 20.8 %reduce-scatter.16.cloned.1.call-done = bf16[512,64]{0,1:T(8,128)(2,1)} async-done(((bf16[2048,64]{0,1:T(8,128)(2,1)}), bf16[512,64]{0,1:T(8,128)(2,1)}) %reduce-scatter.16.cloned.1.call-update) | async-done | bytes 65552 | tf_op jit(solution)/shard_map/reduce_scatter | solution.py:285
  1164.7 21.0 %reduce-scatter.14.cloned.1.call-done = bf16[512,64]{0,1:T(8,128)(2,1)} async-done(((bf16[2048,64]{0,1:T(8,128)(2,1)}), bf16[512,64]{0,1:T(8,128)(2,1)}) %reduce-scatter.14.cloned.1.call-update) | async-done | bytes 65552 | tf_op jit(solution)/shard_map/reduce_scatter | solution.py:282
  1187.2 331.0 %all-reduce.12.cloned.1.call-done = (bf16[1280,2048]{1,0:T(8,128)(2,1)}, bf16[1280,2048]{1,0:T(8,128)(2,1)}) async-done(((bf16[1280,2048]{1,0:T(8,128)(2,1)}, bf16[1280,2048]{1,0:T(8,128)(2,1)}), (bf16[1280,2048]{1,0:T(8,128)(2,1)}, bf16[1280,2048]{1,0:T(8,128)(2,1)})) %all-reduce.12.cloned.1.call-update) | async-done | bytes 10485776 | tf_op jit(solution)/shard_map/psum | solution.py:195
  1518.2 10.0 add_convert_fusion.2
  1543.9 19.1 %psum.40 = bf16[512]{0:T(512)(128)(2,1)S(1)} all-reduce(bf16[512]{0:T(512)(128)(2,1)S(1)} %dynamic-slice.3), channel_id=1, replica_groups=mesh['batch'=4,'head'=8] {'head'}, use_global_device_ids=true, to_apply=%region_61.62 | all-reduce | flops 512 | bytes 2048 | tf_op jit(solution)/shard_map/psum | solution.py:266
  1563.6 10.8 fusion.119
  (209 shorter events, 252.7 us)
Async XLA Ops:
  7.2 85.5 %all-gather.8.cloned.1.call-start = ((), (), s32[]{:S(2)}) async-start(), calls=%async_computation.9 | async-start | bytes 3276800 | tf_op jit(solution)/shard_map/all_gather | solution.py:112
  7.2 23.8 %copy-start.2 = (bf16[1280,2048]{1,0:T(8,128)(2,1)S(1)}, bf16[1280,2048]{1,0:T(8,128)(2,1)}, u32[]{:S(2)}) copy-start(bf16[1280,2048]{1,0:T(8,128)(2,1)} %param.45) | copy-start | bytes 15728644
  14.3 18.0 %copy-start.21 = (f32[4,1,512]{2,1,0:T(1,128)}, f32[4,1,512]{2,1,0:T(1,128)S(1)}, u32[]{:S(2)}) copy-start(f32[4,1,512]{2,1,0:T(1,128)S(1)} %convert_element_type.276) | copy-start | bytes 24580
  18.5 18.0 %copy-start.23 = (f32[1280]{0:T(1024)}, f32[1280]{0:T(1024)S(1)}, u32[]{:S(2)}) copy-start(f32[1280]{0:T(1024)S(1)} %get-tuple-element.735) | copy-start | bytes 15364
  25.0 11.6 copy-start.17
  34.6 13.1 copy-start.20
  34.7 27.8 %copy-start.25 = (bf16[512,128]{1,0:T(8,128)(2,1)S(1)}, bf16[512,128]{1,0:T(8,128)(2,1)}, u32[]{:S(2)}) copy-start(bf16[512,128]{1,0:T(8,128)(2,1)} %param.48) | copy-start | bytes 393220
  34.7 38.2 %copy-start.26 = (bf16[512,128]{1,0:T(8,128)(2,1)S(1)}, bf16[512,128]{1,0:T(8,128)(2,1)}, u32[]{:S(2)}) copy-start(bf16[512,128]{1,0:T(8,128)(2,1)} %param.51) | copy-start | bytes 393220
  34.7 46.0 %copy-start.27 = (bf16[128,512]{1,0:T(8,128)(2,1)S(1)}, bf16[128,512]{1,0:T(8,128)(2,1)}, u32[]{:S(2)}) copy-start(bf16[128,512]{1,0:T(8,128)(2,1)} %param.52) | copy-start | bytes 393220
  36.6 10.0 collective-permute-start
  47.7 455.9 %all-reduce.8.cloned.1.call-start = ((), (), s32[]{:S(2)}) async-start(), calls=%async_computation.10 | async-start | bytes 20971520 | tf_op jit(solution)/shard_map/psum | solution.py:177
  72.9 15.0 copy-start.11
  111.1 11.6 copy-start.5
  122.7 410.1 %all-gather.12.cloned.1.call-start = ((), (), s32[]{:S(2)}) async-start(), calls=%async_computation.12 | async-start | bytes 3932160 | tf_op jit(solution)/shard_map/all_gather | solution.py:69
  123.5 439.4 %all-gather.10.cloned.1.call-start = ((), (), s32[]{:S(2)}) async-start(), calls=%async_computation.11 | async-start | bytes 3932160 | tf_op jit(solution)/shard_map/all_gather | solution.py:68
  124.0 468.9 %all-gather.14.cloned.1.call-start = ((), (), s32[]{:S(2)}) async-start(), calls=%async_computation.13 | async-start | bytes 3932160 | tf_op jit(solution)/shard_map/all_gather | solution.py:70
  124.6 678.3 %all-reduce.10.cloned.1.call-start = ((), (), s32[]{:S(2)}) async-start(), calls=%async_computation.14 | async-start | bytes 10485760 | tf_op jit(solution)/shard_map/psum | solution.py:197
  592.9 13.6 copy-start.32
  618.7 327.7 %reduce-scatter.10.cloned.1.call-start = ((), (), s32[]{:S(2)}) async-start(), calls=%async_computation.15 | async-start | bytes 3276800 | tf_op jit(solution)/shard_map/reduce_scatter | solution.py:242
  855.8 142.7 %reduce-scatter.26.cloned.1.call-start = ((), (), s32[]{:S(2)}) async-start(), calls=%async_computation.23 | async-start | bytes 3932160 | tf_op jit(solution)/shard_map/reduce_scatter | solution.py:303
  864.2 163.5 %reduce-scatter.24.cloned.1.call-start = ((), (), s32[]{:S(2)}) async-start(), calls=%async_computation.22 | async-start | bytes 3932160 | tf_op jit(solution)/shard_map/reduce_scatter | solution.py:300
  873.5 194.5 %reduce-scatter.22.cloned.1.call-start = ((), (), s32[]{:S(2)}) async-start(), calls=%async_computation.21 | async-start | bytes 3932160 | tf_op jit(solution)/shard_map/reduce_scatter | solution.py:297
  882.7 209.7 %reduce-scatter.20.cloned.1.call-start = ((), (), s32[]{:S(2)}) async-start(), calls=%async_computation.20 | async-start | bytes 655360 | tf_op jit(solution)/shard_map/reduce_scatter | solution.py:291
  888.5 227.9 %reduce-scatter.18.cloned.1.call-start = ((), (), s32[]{:S(2)}) async-start(), calls=%async_computation.19 | async-start | bytes 655360 | tf_op jit(solution)/shard_map/reduce_scatter | solution.py:288
  893.4 247.3 %reduce-scatter.12.cloned.1.call-start = ((), (), s32[]{:S(2)}) async-start(), calls=%async_computation.16 | async-start | bytes 655360 | tf_op jit(solution)/shard_map/reduce_scatter | solution.py:279
  901.5 51.5 %copy-start.12 = (bf16[2048,128]{1,0:T(8,128)(2,1)S(1)}, bf16[2048,128]{1,0:T(8,128)(2,1)}, u32[]{:S(2)}) copy-start(bf16[2048,128]{1,0:T(8,128)(2,1)} %copy-done.11) | copy-start | bytes 1572868
  946.4 16.7 %collective-permute-start.1 = (bf16[1280,256]{0,1:T(8,128)(2,1)}, bf16[1280,256]{0,1:T(8,128)(2,1)S(1)}, u32[]{:S(2)}, u32[]{:S(2)}) collective-permute-start(bf16[1280,256]{0,1:T(8,128)(2,1)} %reduce-scatter.10.cloned.1.call-done), channel_id=1, source_target_pairs={{0,1},{1,0},{2,3},{3,2},{4,5},{5,4},{6,7},{7,6},{8,9},{9,8},{10,11... | collective-permute-start | bytes 1966088 | tf_op jit(solution)/shard_map/ppermute | solution.py:18
  952.9 10.2 copy-start.19
  952.9 210.2 %reduce-scatter.16.cloned.1.call-start = ((), (), s32[]{:S(2)}) async-start(), calls=%async_computation.18 | async-start | bytes 327680 | tf_op jit(solution)/shard_map/reduce_scatter | solution.py:285
  972.9 212.8 %reduce-scatter.14.cloned.1.call-start = ((), (), s32[]{:S(2)}) async-start(), calls=%async_computation.17 | async-start | bytes 327680 | tf_op jit(solution)/shard_map/reduce_scatter | solution.py:282
  982.8 535.4 %all-reduce.12.cloned.1.call-start = ((), (), s32[]{:S(2)}) async-start(), calls=%async_computation.24 | async-start | bytes 20971520 | tf_op jit(solution)/shard_map/psum | solution.py:195
  1528.2 35.3 %copy-start.28 = (f32[1280]{0:T(1024)S(1)}, f32[1280]{0:T(1024)}, u32[]{:S(2)}) copy-start(f32[1280]{0:T(1024)} %get-tuple-element.734) | copy-start | bytes 15364
  (23 other events, 127.6 us)
Sparse Core Ops, SparseCore 0:
  47.8 29.6 all-gather.7
  122.9 380.6 all-reduce.7
  505.2 27.5 all-gather.11
  534.3 28.5 all-gather.9
  564.4 28.5 all-gather.13
  618.9 184.0 all-reduce.9
  855.9 90.4 reduce-scatter.9
  948.9 37.9 reduce-scatter.25
  989.6 37.9 reduce-scatter.23
  1030.0 37.9 reduce-scatter.21
  1070.7 21.6 reduce-scatter.19
  1094.7 21.6 reduce-scatter.17
  1119.1 21.6 reduce-scatter.11
  1143.1 20.0 reduce-scatter.15
  1165.6 20.0 reduce-scatter.13
  1190.2 327.9 all-reduce.11
where the time goes:
time: 1590 us; the launch traced here: 1580 us
  waiting for transfers between devices  1120 us (70%)
  matrix products  175 us (11%)
  blocking collectives  133 us (8%)
  other arithmetic  95.2 us (6%)
  local copies, waits for them, and re-layouts  25 us (2%)
  between operations  23.4 us (1%)
    psum x1, waiting for transfers between devices, per_device(): lax.psum(mlp_part.astype(jnp.bfloat16), 'head').astype(jnp.float32)  331 us
    psum x1, waiting for transfers between devices, per_device(): resid = inputs + lax.psum(attn_part, 'head')  322 us
    psum x1, waiting for transfers between devices, per_device(): lax.psum(dn2_part.astype(jnp.bfloat16), 'head').astype(jnp.float32)  184 us
    dot_general x13, matrix products, cols_inner(): lax.dot_general(left, right, (((1,), (1,)), ((), ())), preferred_element_...  73.1 us
    all_gather x1, blocking collectives, per_device(): lax.all_gather(norm2_gain, 'batch', axis=0, tiled=True)  57.2 us
    dot_general x10, matrix products, rows_inner(): lax.dot_general(left, right, (((0,), (0,)), ((), ())), preferred_element_...  51.8 us
    dot_general x9, matrix products, matmul(): return jnp.dot(left, right, preferred_element_type=jnp.float32)  50.3 us
    reduce_scatter x1, waiting for transfers between devices, per_device(): lax.psum_scatter(d_kv_all.astype(jnp.bfloat16), 'batch', scatter_dimensio...  44.9 us
  transfers between devices with their start and end apart: 18, of which 16 were waited for; matrix products, arithmetic and copies ran while one was open for 9% of the time, Pallas kernels for 0%

commit v1 on v0

--- a/solution.py
+++ b/solution.py
@@ -174,7 +174,7 @@
     gate_vals = jax.nn.sigmoid(matmul(normed_one, gate_full))
     mixed = (attended * gate_vals).astype(jnp.bfloat16)
     attn_part = matmul(mixed, out_full)
-    resid = inputs + lax.psum(attn_part, "head")
+    resid = inputs + jax.lax.all_gather(attn_part, "head").sum(axis=0)
     recip_two = rms_scale(resid)
     normed_two = (resid * recip_two * gain_two).astype(jnp.bfloat16)
     gate_pre = matmul(normed_two, mgate_full)

time: 1590 us -> 2850 us (1.79)
  waiting for transfers between devices: 1120 us -> 2340 us
  other arithmetic: 95.2 us -> 127 us
    all_gather x0 -> x1, waiting for transfers between devices: none -> 1580 us  [per_device(): resid = inputs + jax.lax.all_gather(attn_part, 'head').sum(axis=0)]
    psum x1 -> x0, waiting for transfers between devices: 322 us -> none  [per_device(): resid = inputs + lax.psum(attn_part, 'head')]
    reduce_scatter x1, waiting for transfers between devices: 0.02 us -> 38.9 us  [per_device(): lax.psum_scatter(d_down.astype(jnp.bfloat16), 'batch', scatter_dimension=...]
    reduce_scatter x1, waiting for transfers between devices: 38 us -> 0.02 us  [per_device(): lax.psum_scatter(d_mgate.astype(jnp.bfloat16), 'batch', scatter_dimension...]
    reduce_sum x0 -> x1, other arithmetic: none -> 31.7 us  [per_device(): resid = inputs + jax.lax.all_gather(attn_part, 'head').sum(axis=0)]
  transfers between devices with their start and end apart: 18 -> 18, of which waited for: 16 -> 14; matrix products, arithmetic and copies ran while one was open for 9% -> 6% of each run, Pallas kernels for 0% -> 0%
where the time goes in v1:
time: 2850 us; the launch traced here: 2840 us
  waiting for transfers between devices  2340 us (82%)
  matrix products  176 us (6%)
  blocking collectives  132 us (5%)
  other arithmetic  127 us (4%)
    all_gather x1, waiting for transfers between devices, per_device(): resid = inputs + jax.lax.all_gather(attn_part, 'head').sum(axis=0)  1580 us
    psum x1, waiting for transfers between devices, per_device(): lax.psum(mlp_part.astype(jnp.bfloat16), 'head').astype(jnp.float32)  332 us
    psum x1, waiting for transfers between devices, per_device(): lax.psum(dn2_part.astype(jnp.bfloat16), 'head').astype(jnp.float32)  184 us
    dot_general x13, matrix products, cols_inner(): lax.dot_general(left, right, (((1,), (1,)), ((), ())), preferred_element_...  72.6 us
    all_gather x1, blocking collectives, per_device(): lax.all_gather(norm2_gain, 'batch', axis=0, tiled=True)  57 us
  transfers between devices with their start and end apart: 18, of which 14 were waited for; matrix products, arithmetic and copies ran while one was open for 6% of the time, Pallas kernels for 0%

profile of v1, /device:TPU:0, one launch (start us, length us, event | category | flops | bytes accessed | tf_op | source)
XLA Modules:
  0.0 2835.1 jit_solution(5410276101814420701)
XLA Ops:
  38.2 8.3 collective-permute-done
  62.3 10.5 all_gather.47
  92.6 9.2 conditional.16
  124.3 57.0 %all-gather.3 = bf16[4,1,512]{2,1,0:T(2,128)(2,1)S(1)} all-gather(bf16[1,1,512]{2,1,0:T(2,128)(2,1)S(1)} %reshape.213), channel_id=1, replica_groups=mesh['batch'=4,'head'=8] {'batch'}, dimensions={0}, use_global_device_ids=true | all-gather | bytes 5120 | tf_op jit(solution)/shard_map/all_gather | solution.py:67
  181.3 1576.0 %all-gather.18.cloned.1.call-done = f32[10240,2048]{1,0:T(8,128)} async-done(((f32[1280,2048]{1,0:T(8,128)}), f32[10240,2048]{1,0:T(8,128)}) %all-gather.18.cloned.1.call-update) | async-done | bytes 83886096 | tf_op jit(solution)/shard_map/all_gather | solution.py:177
  1757.3 31.7 %reduce_sum.136 = f32[1280,2048]{1,0:T(8,128)} reduce(f32[8,1280,2048]{2,1,0:T(8,128)} %bitcast.6, f32[]{:T(128)} %constant.167.clone.1), dimensions={0}, to_apply=%region_25.26 | reduce | flops 18350080 | bytes 94371840 | tf_op jit(solution)/shard_map/reduce_sum | solution.py:177
  1789.1 10.9 multiply_reduce_fusion
  1807.2 9.6 fusion.160
  1817.4 9.6 fusion.161
  1827.0 20.4 all-gather.16.cloned.1.call-done
  1847.4 13.6 multiply_convert_fusion.1
  1873.2 184.1 %all-reduce.7.cloned.1.call-done = bf16[1280,2048]{1,0:T(8,128)(2,1)} async-done(((bf16[1280,2048]{1,0:T(8,128)(2,1)}), bf16[1280,2048]{1,0:T(8,128)(2,1)}) %all-reduce.7.cloned.1.call-update) | async-done | bytes 5242896 | tf_op jit(solution)/shard_map/psum | solution.py:197
  2057.4 9.4 fusion.124
  2079.0 8.2 conditional.24
  2087.7 12.9 conditional.28
  2110.1 8.4 convolution_convert_fusion.3
  2118.6 9.2 convolution_convert_fusion.2
  2144.1 9.0 convolution_convert_fusion.1
  2153.2 46.7 %reduce-scatter.10.cloned.1.call-done = bf16[1280,256]{0,1:T(8,128)(2,1)} async-done(((bf16[5120,256]{0,1:T(8,128)(2,1)}), bf16[1280,256]{0,1:T(8,128)(2,1)}) %reduce-scatter.10.cloned.1.call-update) | async-done | bytes 655376 | tf_op jit(solution)/shard_map/reduce_scatter | solution.py:242
  2201.4 9.1 convolution_convert_fusion
  2237.0 13.4 add_convert_fusion
  2254.8 26.3 reduce-scatter.24.cloned.1.call-done
  2283.5 21.8 reduce-scatter.20.cloned.1.call-done
  2306.9 22.6 reduce-scatter.12.cloned.1.call-done
  2331.1 22.5 reduce-scatter.18.cloned.1.call-done
  2355.2 38.9 %reduce-scatter.26.cloned.1.call-done = bf16[768,512]{1,0:T(8,128)(2,1)} async-done(((bf16[768,2048]{1,0:T(8,128)(2,1)}), bf16[768,512]{1,0:T(8,128)(2,1)}) %reduce-scatter.26.cloned.1.call-update) | async-done | bytes 786448 | tf_op jit(solution)/shard_map/reduce_scatter | solution.py:303
  2396.6 20.1 reduce-scatter.14.cloned.1.call-done
  2418.2 20.8 reduce-scatter.16.cloned.1.call-done
  2440.5 331.6 %all-reduce.9.cloned.1.call-done = (bf16[1280,2048]{1,0:T(8,128)(2,1)}, bf16[1280,2048]{1,0:T(8,128)(2,1)}) async-done(((bf16[1280,2048]{1,0:T(8,128)(2,1)}, bf16[1280,2048]{1,0:T(8,128)(2,1)}), (bf16[1280,2048]{1,0:T(8,128)(2,1)}, bf16[1280,2048]{1,0:T(8,128)(2,1)})) %all-reduce.9.cloned.1.call-update) | async-done | bytes 10485776 | tf_op jit(solution)/shard_map/psum | solution.py:195
  2787.1 19.1 psum.32
  2807.4 10.0 add_convert_fusion.2
  2817.5 10.9 fusion.119
  (210 shorter events, 240.2 us)
Async XLA Ops:
  7.2 85.4 %all-gather.10.cloned.1.call-start = ((), (), s32[]{:S(2)}) async-start(), calls=%async_computation.9 | async-start | bytes 3276800 | tf_op jit(solution)/shard_map/all_gather | solution.py:112
  7.2 23.7 copy-start.2
  11.6 24.9 copy-start.21
  18.4 18.1 copy-start.23
  24.8 11.6 copy-start.17
  34.5 13.1 copy-start.20
  34.5 27.8 copy-start.25
  34.5 38.3 %copy-start.26 = (bf16[512,128]{1,0:T(8,128)(2,1)S(1)}, bf16[512,128]{1,0:T(8,128)(2,1)}, u32[]{:S(2)}) copy-start(bf16[512,128]{1,0:T(8,128)(2,1)} %param.51) | copy-start | bytes 393220
  34.5 46.0 %copy-start.27 = (bf16[128,512]{1,0:T(8,128)(2,1)S(1)}, bf16[128,512]{1,0:T(8,128)(2,1)}, u32[]{:S(2)}) copy-start(bf16[128,512]{1,0:T(8,128)(2,1)} %param.52) | copy-start | bytes 393220
  36.5 10.0 collective-permute-start
  47.6 1709.7 %all-gather.18.cloned.1.call-start = ((), (), s32[]{:S(2)}) async-start(), calls=%async_computation.23 | async-start | bytes 94371840 | tf_op jit(solution)/shard_map/all_gather | solution.py:177
  72.8 19.7 copy-start.11
  110.7 11.6 copy-start.5
  122.3 1684.9 %all-gather.12.cloned.1.call-start = ((), (), s32[]{:S(2)}) async-start(), calls=%async_computation.10 | async-start | bytes 3932160 | tf_op jit(solution)/shard_map/all_gather | solution.py:68
  123.1 1694.3 %all-gather.14.cloned.1.call-start = ((), (), s32[]{:S(2)}) async-start(), calls=%async_computation.11 | async-start | bytes 3932160 | tf_op jit(solution)/shard_map/all_gather | solution.py:69
  123.7 1723.7 %all-gather.16.cloned.1.call-start = ((), (), s32[]{:S(2)}) async-start(), calls=%async_computation.12 | async-start | bytes 3932160 | tf_op jit(solution)/shard_map/all_gather | solution.py:70
  124.2 1933.1 %all-reduce.7.cloned.1.call-start = ((), (), s32[]{:S(2)}) async-start(), calls=%async_computation.13 | async-start | bytes 10485760 | tf_op jit(solution)/shard_map/psum | solution.py:197
  1847.4 13.6 copy-start.31
  1873.2 326.7 %reduce-scatter.10.cloned.1.call-start = ((), (), s32[]{:S(2)}) async-start(), calls=%async_computation.14 | async-start | bytes 3276800 | tf_op jit(solution)/shard_map/reduce_scatter | solution.py:242
  2105.7 146.7 %reduce-scatter.22.cloned.1.call-start = ((), (), s32[]{:S(2)}) async-start(), calls=%async_computation.20 | async-start | bytes 3932160 | tf_op jit(solution)/shard_map/reduce_scatter | solution.py:297
  2118.6 162.5 %reduce-scatter.24.cloned.1.call-start = ((), (), s32[]{:S(2)}) async-start(), calls=%async_computation.21 | async-start | bytes 3932160 | tf_op jit(solution)/shard_map/reduce_scatter | solution.py:300
  2127.8 177.4 %reduce-scatter.20.cloned.1.call-start = ((), (), s32[]{:S(2)}) async-start(), calls=%async_computation.19 | async-start | bytes 655360 | tf_op jit(solution)/shard_map/reduce_scatter | solution.py:291
  2133.6 195.9 %reduce-scatter.12.cloned.1.call-start = ((), (), s32[]{:S(2)}) async-start(), calls=%async_computation.15 | async-start | bytes 655360 | tf_op jit(solution)/shard_map/reduce_scatter | solution.py:279
  2138.7 214.9 %reduce-scatter.18.cloned.1.call-start = ((), (), s32[]{:S(2)}) async-start(), calls=%async_computation.18 | async-start | bytes 655360 | tf_op jit(solution)/shard_map/reduce_scatter | solution.py:288
  2143.7 250.4 %reduce-scatter.26.cloned.1.call-start = ((), (), s32[]{:S(2)}) async-start(), calls=%async_computation.22 | async-start | bytes 3932160 | tf_op jit(solution)/shard_map/reduce_scatter | solution.py:303
  2153.1 57.3 %copy-start.12 = (bf16[2048,128]{1,0:T(8,128)(2,1)S(1)}, bf16[2048,128]{1,0:T(8,128)(2,1)}, u32[]{:S(2)}) copy-start(bf16[2048,128]{1,0:T(8,128)(2,1)} %copy-done.11) | copy-start | bytes 1572868
  2153.1 263.5 %reduce-scatter.14.cloned.1.call-start = ((), (), s32[]{:S(2)}) async-start(), calls=%async_computation.16 | async-start | bytes 327680 | tf_op jit(solution)/shard_map/reduce_scatter | solution.py:282
  2199.9 17.2 collective-permute-start.1
  2227.0 212.0 %reduce-scatter.16.cloned.1.call-start = ((), (), s32[]{:S(2)}) async-start(), calls=%async_computation.17 | async-start | bytes 327680 | tf_op jit(solution)/shard_map/reduce_scatter | solution.py:285
  2237.0 535.1 %all-reduce.9.cloned.1.call-start = ((), (), s32[]{:S(2)}) async-start(), calls=%async_computation.24 | async-start | bytes 20971520 | tf_op jit(solution)/shard_map/psum | solution.py:195
  2250.5 521.6 %copy-start.22 = (f32[1280]{0:T(1024)S(1)}, f32[1280]{0:T(1024)}, u32[]{:S(2)}) copy-start(f32[1280]{0:T(1024)} %copy-done.21) | copy-start | bytes 15364
  2250.5 521.6 %copy-start.24 = (f32[4,1,512]{2,1,0:T(1,128)S(1)}, f32[4,1,512]{2,1,0:T(1,128)}, u32[]{:S(2)}) copy-start(f32[4,1,512]{2,1,0:T(1,128)} %copy-done.23) | copy-start | bytes 24580
  (23 other events, 122.6 us)
Sparse Core Ops, SparseCore 0:
  47.7 29.6 all-gather.9
  122.5 1634.8 all-gather.17
  1758.9 28.4 all-gather.11
  1788.8 28.5 all-gather.13
  1818.8 28.5 all-gather.15
  1873.3 184.0 all-reduce.6
  2105.8 94.0 reduce-scatter.9
  2202.6 37.9 reduce-scatter.21
  2243.1 37.9 reduce-scatter.23
  2283.6 21.6 reduce-scatter.19
  2307.7 21.6 reduce-scatter.11
  2331.9 21.6 reduce-scatter.17
  2356.1 37.9 reduce-scatter.25
  2396.6 20.0 reduce-scatter.13
  2419.0 20.0 reduce-scatter.15
  2444.0 327.9 all-reduce.8
